TPU v7x, 32 devices: a whole 2x2x4 slice. The times are simulated.
32 devices in a mesh: loop: 8 (over y, x, core), tp: 4 (over z).
Axes of the slice: x: 2, y: 2, z: 4, core: 2. Of those that a mesh axis runs over, the one named last changes fastest.
Arguments:
- tokens: bfloat16 [2048, 4096], P('loop', 'tp'), may hold values from -6 to 6
- out_grad: bfloat16 [2048, 6144], P('loop', 'tp'), may hold values from -6 to 6
- qkv_weight: bfloat16 [3, 4096, 6144], P(None, 'loop', 'tp'), may hold values from -0.09375 to 0.09375
- dest_row: int32 [2048], P('loop'), may hold values from 0 to 383, as said below
- loop_modality: int32 [8], replicated, may hold values from 0 to 2, as said below
Outputs:
- projected: bfloat16 [2048, 6144], P('loop', 'tp')
- input_grad: bfloat16 [2048, 4096], P('loop', 'tp')
- weight_grad: bfloat16 [3, 4096, 6144], P(None, 'loop', 'tp')
Inputs may be any that keep to these rules, and one draw needn't show every extreme that they name: `dest_row`: within each aligned block of 256 tokens the values are distinct, so at most 48 tokens of one block name one loop; in every draw some loop is named by exactly 48 tokens of every block. `loop_modality`: A quarter of the loops hold 0, half hold 1, a quarter hold 2.
All inputs are finite; a program needn't handle non-finite values.
Results may differ from a plain program's by a relative error of at most 0.014.
Values may be sent and summed in bfloat16 or wider, within the bound.
No kernel may reach another device: no remote copies, remote signals or barrier semaphores. Data moves between devices by JAX's collectives and lax.ppermute only.
A program may use at most 128 MiB of HBM per device.

v0:
```python
import math
import jax
import jax.numpy as jnp
from jax import lax
from jax.sharding import PartitionSpec as P


def per_device(tokens, out_grad, qkv_weight, dest_row, loop_modality):
    loop_count = lax.axis_size("loop")
    row_count, feature_part = tokens.shape
    kinds, block_rows, column_count = qkv_weight.shape
    capacity = 3 * row_count // (2 * loop_count)
    grad_scale = 1.0 / math.sqrt(row_count * loop_count)
    own_kind = loop_modality[dest_row // capacity]
    kind_of = lax.all_gather(own_kind, "loop", axis=0, tiled=True)
    grads = lax.all_gather(out_grad, "loop", axis=0, tiled=True)
    features = lax.all_gather(tokens, "tp", axis=1, tiled=True)
    rows = lax.all_to_all(features, "loop", split_axis=1, concat_axis=0, tiled=True)
    masks = [(kind_of == kind)[:, None] for kind in range(kinds)]
    term = sum(
        (
            lax.dot_general(
                jnp.where(masks[kind], grads, 0),
                qkv_weight[kind],
                (((1,), (1,)), ((), ())),
                preferred_element_type=jnp.float32,
            )
            for kind in range(kinds)
        )
    ).astype(jnp.bfloat16)
    term = lax.all_to_all(term, "loop", split_axis=0, concat_axis=1, tiled=True)
    input_grad = lax.psum_scatter(term, "tp", scatter_dimension=1, tiled=True)
    partial = sum(
        (
            jnp.dot(
                jnp.where(masks[kind], rows, 0),
                qkv_weight[kind],
                preferred_element_type=jnp.float32,
            )
            for kind in range(kinds)
        )
    ).astype(jnp.bfloat16)
    projected = lax.psum_scatter(partial, "loop", scatter_dimension=0, tiled=True)
    weight_grad = jnp.stack(
        [
            (
                lax.dot_general(
                    jnp.where(masks[kind], rows, 0),
                    grads,
                    (((0,), (0,)), ((), ())),
                    preferred_element_type=jnp.float32,
                )
                * grad_scale
            ).astype(jnp.bfloat16)
            for kind in range(kinds)
        ]
    )
    return (projected, input_grad, weight_grad)


def solution(mesh):
    placed = (P("loop", "tp"), P("loop", "tp"), P(None, "loop", "tp"), P("loop"), P())
    return jax.shard_map(
        per_device,
        mesh=mesh,
        in_specs=placed,
        out_specs=(P("loop", "tp"), P("loop", "tp"), P(None, "loop", "tp")),
        check_vma=False,
    )
```

profile of v0, /device:TPU:0, one launch (start us, length us, event | category | flops | bytes accessed | tf_op | source)
XLA Modules:
  0.0 278.5 jit_solution(15667492491029857206)
XLA Ops:
  7.2 2.0 copy.17
  10.0 48.5 %all-gather.5.cloned.1.call-done = bf16[256,4096]{0,1:T(8,128)(2,1)} async-done(((bf16[256,1024]{0,1:T(8,128)(2,1)}), bf16[256,4096]{0,1:T(8,128)(2,1)}) %all-gather.5.cloned.1.call-update) | async-done | bytes 2097168 | tf_op jit(solution)/shard_map/all_gather | solution.py:17
  58.5 3.7 %all-to-all-start = ((bf16[256,8,512]{0,2,1:T(8,128)(2,1)}), bf16[256,8,512]{0,2,1:T(8,128)(2,1)S(1)}, u32[]{:S(2)}, u32[]{:S(2)}) async-start(bf16[256,8,512]{0,2,1:T(8,128)(2,1)} %bitcast.68), calls=%async_computation | async-start | bytes 4194304 | tf_op jit(solution)/shard_map/all_to_all | solution.py:18
  63.0 5.2 %compare_select_fusion.1 = s32[256]{0:T(256)S(1)} fusion(s32[256]{0:T(256)S(1)} %copy-done.3, s32[]{:T(128)} %bitcast, s32[]{:T(128)} %bitcast.1, s32[]{:T(128)} %bitcast.2, s32[]{:T(128)} %bitcast.3, s32[]{:T(128)} %bitcast.4, s32[]{:T(128)} %bitcast.5, s32[]{:T(128)} %bitcast.6, s32[]{:T(128)} %bitcast.7), kind=kLoop, calls=%fused_computation.48 | loop fusion | flops 6400 | bytes 2080 | tf_op jit(solution)/shard_map/gather | solution.py:14
  68.1 32.2 %all-gather.1 = s32[8,1,256]{2,1,0:T(1,128)S(1)} all-gather(s32[1,1,256]{2,1,0:T(1,128)S(1)} %bitcast.75), channel_id=2, replica_groups=mesh['loop'=8,'tp'=4] {'loop'}, dimensions={0}, use_global_device_ids=true | all-gather | bytes 9216 | tf_op jit(solution)/shard_map/all_gather | solution.py:15
  100.3 2.8 %broadcast_select_fusion = (bf16[8,256,512]{1,2,0:T(8,128)(2,1)}, bf16[8,256,512]{1,2,0:T(8,128)(2,1)}, bf16[8,256,512]{1,2,0:T(8,128)(2,1)}) fusion(pred[8,256]{1,0:T(8,128)(4,1)S(1)} %bitcast.72, bf16[256,8,512]{0,2,1:T(8,128)(2,1)S(1)} %all-to-all-done, pred[8,256]{1,0:T(8,128)(4,1)S(1)} %bitcast.74, pred[8,256]{1,0:T(8,128)(4,1)S(1)} %bitcast.73), kind=kLoop, calls=%fused_computation.27 | loop fusion | flops 3145728 | bytes 8394752 | tf_op jit(solution)/shard_map/jit(_where)/select_n | solution.py:36
  103.2 3.9 %copy.20 = bf16[8,256,512]{2,1,0:T(8,128)(2,1)} copy(bf16[8,256,512]{1,2,0:T(8,128)(2,1)} %get-tuple-element.8) | data formatting | bytes 4194304 | tf_op jit(solution)/shard_map/jit(_where)/select_n | solution.py:36
  107.1 4.0 %copy.18 = bf16[8,256,512]{2,1,0:T(8,128)(2,1)} copy(bf16[8,256,512]{1,2,0:T(8,128)(2,1)} %get-tuple-element.7) | data formatting | bytes 4194304 | tf_op jit(solution)/shard_map/jit(_where)/select_n | solution.py:36
  111.1 3.9 %copy.22 = bf16[8,256,512]{2,1,0:T(8,128)(2,1)} copy(bf16[8,256,512]{1,2,0:T(8,128)(2,1)} %get-tuple-element.6) | data formatting | bytes 4194304 | tf_op jit(solution)/shard_map/jit(_where)/select_n | solution.py:36
  115.0 10.2 %fusion.23 = f32[2048,1536]{1,0:T(8,128)} fusion(bf16[2048,512]{1,0:T(8,128)(2,1)} %bitcast.69, bf16[3,512,1536]{2,1,0:T(8,128)(2,1)} %param.7), kind=kOutput, calls=%fused_computation.33 | convolution fusion | flops 3221225472 | bytes 16252928 | tf_op jit(solution)/shard_map/dot_general | solution.py:35
  125.2 7.8 %fusion.26 = f32[2048,1536]{1,0:T(8,128)} fusion(bf16[2048,512]{1,0:T(8,128)(2,1)S(1)} %bitcast.70, bf16[3,512,1536]{2,1,0:T(8,128)(2,1)} %param.7), kind=kOutput, calls=%fused_computation.36 | convolution fusion | flops 3221225472 | bytes 16252928 | tf_op jit(solution)/shard_map/dot_general | solution.py:35
  133.0 13.3 %add_convert_fusion = bf16[2048,1536]{1,0:T(8,128)(2,1)} fusion(f32[2048,1536]{1,0:T(8,128)} %fusion.26, f32[2048,1536]{1,0:T(8,128)} %fusion.23, bf16[2048,512]{1,0:T(8,128)(2,1)S(1)} %bitcast.65, bf16[3,512,1536]{2,1,0:T(8,128)(2,1)} %param.7), kind=kOutput, calls=%fused_computation | convolution fusion | flops 3230662656 | bytes 35127296 | tf_op jit(solution)/shard_map/dot_general | solution.py:35
  146.7 6.3 %fusion = f32[2048,512]{1,0:T(8,128)S(1)} fusion(bf16[2048,1536]{1,0:T(8,128)(2,1)} %all-gather.7.cloned.1.call-done, pred[2048]{0:T(1024)(128)(4,1)S(1)} %reshape.57, bf16[3,512,1536]{2,1,0:T(8,128)(2,1)} %param.7), kind=kOutput, calls=%fused_computation.1 | convolution fusion | flops 3224371200 | bytes 12060672 | tf_op jit(solution)/shard_map/dot_general | solution.py:22
  153.0 5.2 %fusion.2 = f32[2048,512]{1,0:T(8,128)S(1)} fusion(bf16[2048,1536]{1,0:T(8,128)(2,1)S(1)} %copy-done.4, pred[2048]{0:T(1024)(128)(4,1)S(1)} %reshape.55, bf16[3,512,1536]{2,1,0:T(8,128)(2,1)} %param.7), kind=kOutput, calls=%fused_computation.3 | convolution fusion | flops 3224371200 | bytes 12060672 | tf_op jit(solution)/shard_map/dot_general | solution.py:22
  158.2 5.2 %add_convert_fusion.1 = bf16[2048,512]{1,0:T(8,128)(2,1)S(1)} fusion(f32[2048,512]{1,0:T(8,128)S(1)} %fusion, f32[2048,512]{1,0:T(8,128)S(1)} %fusion.2, bf16[2048,1536]{1,0:T(8,128)(2,1)S(1)} %copy-done.4, pred[2048]{0:T(1024)(128)(4,1)S(1)} %reshape.53, bf16[3,512,1536]{2,1,0:T(8,128)(2,1)} %param.7), kind=kOutput, calls=%fused_computation.11 | convolution fusion | flops 3227516928 | bytes 18352128 | tf_op jit(solution)/shard_map/dot_general | solution.py:22
  163.4 45.9 %all_to_all.38 = bf16[8,256,512]{2,1,0:T(8,128)(2,1)S(1)} all-to-all(bf16[8,256,512]{2,1,0:T(8,128)(2,1)S(1)} %bitcast.71), channel_id=1, replica_groups=mesh['loop'=8,'tp'=4] {'loop'}, dimensions={0} | all-to-all | bytes 4194304 | tf_op jit(solution)/shard_map/all_to_all | solution.py:31
  209.3 1.6 copy.25
  210.9 2.4 copy.24
  213.3 3.7 %bitcast_select_fusion.2 = (bf16[2048,512]{1,0:T(8,128)(2,1)S(1)}, bf16[2048,512]{1,0:T(8,128)(2,1)S(1)}, bf16[2048,512]{1,0:T(8,128)(2,1)S(1)}) fusion(bf16[8,256,512]{2,1,0:T(8,128)(2,1)} %copy.24, pred[2048]{0:T(1024)(128)(4,1)S(1)} %reshape.53, pred[2048]{0:T(1024)(128)(4,1)S(1)} %reshape.55, pred[2048]{0:T(1024)(128)(4,1)S(1)} %reshape.57), kind=kLoop, calls=%fused_computation.26 | loop fusion | flops 3145728 | bytes 8394752 | tf_op jit(solution)/shard_map/jit(_where)/select_n | solution.py:36
  217.0 6.5 %fusion.15 = bf16[1,512,1536]{2,1,0:T(8,128)(2,1)S(1)} fusion(bf16[2048,512]{1,0:T(8,128)(2,1)S(1)} %get-tuple-element.5, bf16[2048,1536]{1,0:T(8,128)(2,1)} %all-gather.7.cloned.1.call-done), kind=kOutput, calls=%fused_computation.21 | convolution fusion | flops 3222798336 | bytes 9961472 | tf_op jit(solution)/shard_map/dot_general | solution.py:47
  223.5 3.6 %fusion.16 = bf16[1,512,1536]{2,1,0:T(8,128)(2,1)S(1)} fusion(bf16[2048,512]{1,0:T(8,128)(2,1)S(1)} %get-tuple-element.4, bf16[2048,1536]{1,0:T(8,128)(2,1)S(1)} %bitcast.77), kind=kOutput, calls=%fused_computation.22 | convolution fusion | flops 3222798336 | bytes 9961472 | tf_op jit(solution)/shard_map/dot_general | solution.py:47
  227.1 3.6 %fusion.17 = bf16[1,512,1536]{2,1,0:T(8,128)(2,1)S(1)} fusion(bf16[2048,512]{1,0:T(8,128)(2,1)S(1)} %get-tuple-element.3, bf16[2048,1536]{1,0:T(8,128)(2,1)S(1)} %bitcast.77), kind=kOutput, calls=%fused_computation.23 | convolution fusion | flops 3222798336 | bytes 9961472 | tf_op jit(solution)/shard_map/dot_general | solution.py:47
  230.7 2.5 pad_maximum_fusion
  233.2 38.8 %reduce-scatter.5.cloned.1.call-done = bf16[256,1024]{1,0:T(8,128)(2,1)} async-done(((bf16[256,4096]{1,0:T(8,128)(2,1)}), bf16[256,1024]{1,0:T(8,128)(2,1)}) %reduce-scatter.5.cloned.1.call-update) | async-done | bytes 524304 | tf_op jit(solution)/shard_map/reduce_scatter | solution.py:32
  (31 shorter events, 1.9 us)
Async XLA Ops:
  7.2 55.1 %copy-start.2 = (s32[8]{0:T(128)S(1)}, s32[8]{0:T(128)}, u32[]{:S(2)}) copy-start(s32[8]{0:T(128)} %param.9) | copy-start | bytes 100
  7.2 55.8 %copy-start.3 = (s32[256]{0:T(256)S(1)}, s32[256]{0:T(256)}, u32[]{:S(2)}) copy-start(s32[256]{0:T(256)} %param.8) | copy-start | bytes 3076
  7.2 51.4 %all-gather.5.cloned.1.call-start = ((), (), s32[]{:S(2)}) async-start(), calls=%async_computation.4 | async-start | bytes 2621440 | tf_op jit(solution)/shard_map/all_gather | solution.py:17
  9.3 137.4 %all-gather.7.cloned.1.call-start = ((), (), s32[]{:S(2)}) async-start(), calls=%async_computation.6 | async-start | bytes 7077888 | tf_op jit(solution)/shard_map/all_gather | solution.py:16
  58.5 41.8 %all-to-all-start = ((bf16[256,8,512]{0,2,1:T(8,128)(2,1)}), bf16[256,8,512]{0,2,1:T(8,128)(2,1)S(1)}, u32[]{:S(2)}, u32[]{:S(2)}) async-start(bf16[256,8,512]{0,2,1:T(8,128)(2,1)} %bitcast.68), calls=%async_computation | async-start | bytes 4194304 | tf_op jit(solution)/shard_map/all_to_all | solution.py:18
  62.2 171.0 %reduce-scatter.3.cloned.1.call-start = ((), (), s32[]{:S(2)}) async-start(), calls=%async_computation.5 | async-start | bytes 7077888 | tf_op jit(solution)/shard_map/reduce_scatter | solution.py:43
  115.0 10.2 %copy-start.1 = (bf16[8,256,512]{2,1,0:T(8,128)(2,1)S(1)}, bf16[8,256,512]{2,1,0:T(8,128)(2,1)}, u32[]{:S(2)}) copy-start(bf16[8,256,512]{2,1,0:T(8,128)(2,1)} %copy.18) | copy-start | bytes 6291460
  125.2 7.9 %copy-start = (bf16[8,256,512]{2,1,0:T(8,128)(2,1)S(1)}, bf16[8,256,512]{2,1,0:T(8,128)(2,1)}, u32[]{:S(2)}) copy-start(bf16[8,256,512]{2,1,0:T(8,128)(2,1)} %copy.22) | copy-start | bytes 6291460
  146.4 125.6 %reduce-scatter.5.cloned.1.call-start = ((), (), s32[]{:S(2)}) async-start(), calls=%async_computation.7 | async-start | bytes 2621440 | tf_op jit(solution)/shard_map/reduce_scatter | solution.py:32
  146.7 6.3 %copy-start.4 = (bf16[2048,1536]{1,0:T(8,128)(2,1)S(1)}, bf16[2048,1536]{1,0:T(8,128)(2,1)}, u32[]{:S(2)}) copy-start(bf16[2048,1536]{1,0:T(8,128)(2,1)} %all-gather.7.cloned.1.call-done) | copy-start | bytes 18874372
  213.3 10.2 %slice-start = ((s8[6291456]{0:T(1024)(128)(4,1)}), s8[4194304]{0:T(1024)(128)(4,1)S(1)}, s32[]{:S(2)}) async-start(s8[6291456]{0:T(1024)(128)(4,1)} %bitcast.76), calls=%async_computation.8 | async-start | bytes 8388608
  217.0 6.5 %slice-start.1 = ((s8[6291456]{0:T(1024)(128)(4,1)}), s8[2097152]{0:T(1024)(128)(4,1)S(1)}, s32[]{:S(2)}) async-start(s8[6291456]{0:T(1024)(128)(4,1)} %bitcast.76), calls=%async_computation.9 | async-start | bytes 4194304
Sparse Core Ops, SparseCore 0:
  10.1 48.3 all-gather.4
  60.4 58.3 all-gather.6
  146.5 79.0 reduce-scatter.2
  228.3 43.6 reduce-scatter.4
where the time goes:
time: 279 us
  waiting for transfers between devices  88.1 us (32%)
  blocking collectives  78.1 us (28%)
  matrix products  61.7 us (22%)
  local copies, waits for them, and re-layouts  18.6 us (7%)
  other arithmetic  14.1 us (5%)
  between operations  13.9 us (5%)
  starting transfers between devices  3.99 us (1%)
    all_gather x1, waiting for transfers between devices, per_device(): features = lax.all_gather(tokens, 'tp', axis=1, tiled=True)  48.5 us
    all_to_all x1, blocking collectives, per_device(): term = lax.all_to_all(term, 'loop', split_axis=0, concat_axis=1, tiled=True)  45.9 us
    reduce_scatter x1, waiting for transfers between devices, per_device(): input_grad = lax.psum_scatter(term, 'tp', scatter_dimension=1, tiled=True)  38.8 us
    all_gather x1, blocking collectives, per_device(): kind_of = lax.all_gather(own_kind, 'loop', axis=0, tiled=True)  32.2 us
    dot_general x3, matrix products, per_device(): jnp.dot(jnp.where(masks[kind], rows, 0), qkv_weight[kind], preferred_elem...  31.3 us
    dot_general x3, matrix products, per_device(): lax.dot_general(jnp.where(masks[kind], grads, 0), qkv_weight[kind], (((1,...  16.7 us
    dot_general x3, matrix products, per_device(): lax.dot_general(jnp.where(masks[kind], rows, 0), grads, (((0,), (0,)), ((...  13.6 us
    select_n x3, local copies, waits for them, and re-layouts, per_device(): jnp.where(masks[kind], rows, 0)  11.8 us
  transfers between devices with their start and end apart: 5, of which 2 were waited for; matrix products, arithmetic and copies ran while one was open for 33% of the time, Pallas kernels for 0%

commit v1 on v0

--- a/solution.py
+++ b/solution.py
@@ -1,8 +1,20 @@
+import functools
 import math
 import jax
 import jax.numpy as jnp
 from jax import lax
 from jax.sharding import PartitionSpec as P
+
+
+def _attach_run(chunk, dim_no, on_dim):
+    all_rows = lax.axis_size("loop")
+    after = jnp.split(chunk, all_rows, axis=dim_no)
+    parts_out = jnp.stack(after, axis=0)
+    plain = lax.all_to_all(parts_out, "loop", 0, 0)
+    return jnp.concatenate(plain, axis=on_dim)
+
+
+obtain_series = functools.partial(_attach_run, dim_no=0, on_dim=1)
 
 
 def per_device(tokens, out_grad, qkv_weight, dest_row, loop_modality):
@@ -28,7 +40,7 @@
             for kind in range(kinds)
         )
     ).astype(jnp.bfloat16)
-    term = lax.all_to_all(term, "loop", split_axis=0, concat_axis=1, tiled=True)
+    term = obtain_series(term)
     input_grad = lax.psum_scatter(term, "tp", scatter_dimension=1, tiled=True)
     partial = sum(
         (

time: 279 us -> 256 us (0.918)
  blocking collectives: 78.1 us -> 10.6 us
  waiting for transfers between devices: 88.1 us -> 116 us
  local copies, waits for them, and re-layouts: 18.6 us -> 30.2 us
  starting transfers between devices: 3.99 us -> 7.55 us
    all_to_all x1 -> x0, blocking collectives: 45.9 us -> none  [per_device(): term = lax.all_to_all(term, 'loop', split_axis=0, concat_axis=1, tiled=True)]
    reduce_scatter x1, waiting for transfers between devices: 38.8 us -> 0.01 us  [per_device(): input_grad = lax.psum_scatter(term, 'tp', scatter_dimension=1, tiled=True)]
    reduce_scatter x1, waiting for transfers between devices: 0.01 us -> 35.2 us  [per_device(): lax.psum_scatter(partial, 'loop', scatter_dimension=0, tiled=True)]
    all_gather x1, waiting for transfers between devices: 0.02 us -> 31.5 us  [per_device(): grads = lax.all_gather(out_grad, 'loop', axis=0, tiled=True)]
    all_gather x1, waiting for transfers between devices: 48.5 us -> 22 us  [per_device(): features = lax.all_gather(tokens, 'tp', axis=1, tiled=True)]
    all_to_all x1, waiting for transfers between devices: 0.01 us -> 22.3 us  [per_device(): lax.all_to_all(features, 'loop', split_axis=1, concat_axis=0, tiled=True)]
    all_gather x1, blocking collectives: 32.2 us -> 10.6 us  [per_device(): kind_of = lax.all_gather(own_kind, 'loop', axis=0, tiled=True)]
    unnamed x15 -> x25, local copies, waits for them, and re-layouts: 2.07 us -> 10.6 us
  transfers between devices with their start and end apart: 5 -> 6, of which waited for: 2 -> 5; matrix products, arithmetic and copies ran while one was open for 33% -> 41% of each run, Pallas kernels for 0% -> 0%
where the time goes in v1:
time: 256 us; the launch traced here: 255 us
  waiting for transfers between devices  116 us (45%)
  matrix products  62.2 us (24%)
  local copies, waits for them, and re-layouts  30.2 us (12%)
  other arithmetic  14.7 us (6%)
  between operations  13.9 us (5%)
  blocking collectives  10.6 us (4%)
  starting transfers between devices  7.55 us (3%)
    reduce_scatter x1, waiting for transfers between devices, per_device(): lax.psum_scatter(partial, 'loop', scatter_dimension=0, tiled=True)  35.2 us
    all_gather x1, waiting for transfers between devices, per_device(): grads = lax.all_gather(out_grad, 'loop', axis=0, tiled=True)  31.5 us
    dot_general x3, matrix products, per_device(): jnp.dot(jnp.where(masks[kind], rows, 0), qkv_weight[kind], preferred_elem...  31.3 us
    all_to_all x1, waiting for transfers between devices, per_device(): lax.all_to_all(features, 'loop', split_axis=1, concat_axis=0, tiled=True)  22.3 us
    all_gather x1, waiting for transfers between devices, per_device(): features = lax.all_gather(tokens, 'tp', axis=1, tiled=True)  22 us
    dot_general x3, matrix products, per_device(): lax.dot_general(jnp.where(masks[kind], grads, 0), qkv_weight[kind], (((1,...  16.4 us
    dot_general x3, matrix products, per_device(): lax.dot_general(jnp.where(masks[kind], rows, 0), grads, (((0,), (0,)), ((...  14.6 us
    select_n x3, local copies, waits for them, and re-layouts, per_device(): jnp.where(masks[kind], rows, 0)  11.8 us
  transfers between devices with their start and end apart: 6, of which 5 were waited for; matrix products, arithmetic and copies ran while one was open for 41% of the time, Pallas kernels for 0%

profile of v1, /device:TPU:0, one launch (start us, length us, event | category | flops | bytes accessed | tf_op | source)
XLA Modules:
  0.0 255.5 jit_solution(1909891860356894327)
XLA Ops:
  10.7 5.2 %compare_select_fusion.1 = s32[256]{0:T(256)S(1)} fusion(s32[256]{0:T(256)S(1)} %copy-done.4, s32[]{:T(128)} %bitcast, s32[]{:T(128)} %bitcast.1, s32[]{:T(128)} %bitcast.2, s32[]{:T(128)} %bitcast.3, s32[]{:T(128)} %bitcast.4, s32[]{:T(128)} %bitcast.5, s32[]{:T(128)} %bitcast.6, s32[]{:T(128)} %bitcast.7), kind=kLoop, calls=%fused_computation.64 | loop fusion | flops 6400 | bytes 2080 | tf_op jit(solution)/shard_map/gather | solution.py:26
  15.9 10.6 %all-gather.1 = s32[8,1,256]{2,1,0:T(1,128)S(1)} all-gather(s32[1,1,256]{2,1,0:T(1,128)S(1)} %bitcast.104), channel_id=2, replica_groups=mesh['loop'=8,'tp'=4] {'loop'}, dimensions={0}, use_global_device_ids=true | all-gather | bytes 9216 | tf_op jit(solution)/shard_map/all_gather | solution.py:27
  26.6 31.5 %all-gather.7.cloned.1.call-done = bf16[2048,1536]{1,0:T(8,128)(2,1)} async-done(((bf16[256,1536]{1,0:T(8,128)(2,1)}), bf16[2048,1536]{1,0:T(8,128)(2,1)}) %all-gather.7.cloned.1.call-update) | async-done | bytes 6291472 | tf_op jit(solution)/shard_map/all_gather | solution.py:28
  58.0 6.3 %fusion = f32[2048,512]{1,0:T(8,128)S(1)} fusion(bf16[2048,1536]{1,0:T(8,128)(2,1)} %all-gather.7.cloned.1.call-done, pred[2048]{0:T(1024)(128)(4,1)S(1)} %reshape.62, bf16[3,512,1536]{2,1,0:T(8,128)(2,1)} %param.7), kind=kOutput, calls=%fused_computation.1 | convolution fusion | flops 3224371200 | bytes 12060672 | tf_op jit(solution)/shard_map/dot_general | solution.py:34
  64.3 5.0 %fusion.2 = f32[2048,512]{1,0:T(8,128)S(1)} fusion(bf16[2048,1536]{1,0:T(8,128)(2,1)S(1)} %copy-done.5, pred[2048]{0:T(1024)(128)(4,1)S(1)} %reshape.60, bf16[3,512,1536]{2,1,0:T(8,128)(2,1)} %param.7), kind=kOutput, calls=%fused_computation.3 | convolution fusion | flops 3224371200 | bytes 12060672 | tf_op jit(solution)/shard_map/dot_general | solution.py:34
  69.3 5.2 %add_convert_fusion.1 = bf16[2048,512]{1,0:T(8,128)(2,1)S(1)} fusion(f32[2048,512]{1,0:T(8,128)S(1)} %fusion, f32[2048,512]{1,0:T(8,128)S(1)} %fusion.2, bf16[2048,1536]{1,0:T(8,128)(2,1)S(1)} %copy-done.5, pred[2048]{0:T(1024)(128)(4,1)S(1)} %reshape.58, bf16[3,512,1536]{2,1,0:T(8,128)(2,1)} %param.7), kind=kOutput, calls=%fused_computation.11 | convolution fusion | flops 3227516928 | bytes 18352128 | tf_op jit(solution)/shard_map/dot_general | solution.py:34
  80.2 3.6 %all-to-all-start.1 = ((bf16[8,256,512]{2,1,0:T(8,128)(2,1)}), bf16[8,256,512]{2,1,0:T(8,128)(2,1)S(1)}, u32[]{:S(2)}, u32[]{:S(2)}) async-start(bf16[8,256,512]{2,1,0:T(8,128)(2,1)} %fusion.34), calls=%async_computation.2 | async-start | bytes 4194304 | tf_op jit(solution)/shard_map/all_to_all | solution.py:13
  83.9 22.0 %all-gather.5.cloned.1.call-done = bf16[256,4096]{0,1:T(8,128)(2,1)} async-done(((bf16[256,1024]{0,1:T(8,128)(2,1)}), bf16[256,4096]{0,1:T(8,128)(2,1)}) %all-gather.5.cloned.1.call-update) | async-done | bytes 2097168 | tf_op jit(solution)/shard_map/all_gather | solution.py:29
  105.9 4.5 %all-to-all-done.1 = bf16[8,256,512]{2,1,0:T(8,128)(2,1)S(1)} async-done(((bf16[8,256,512]{2,1,0:T(8,128)(2,1)}), bf16[8,256,512]{2,1,0:T(8,128)(2,1)S(1)}, u32[]{:S(2)}, u32[]{:S(2)}) %all-to-all-start.1) | async-done | bytes 2097184 | tf_op jit(solution)/shard_map/all_to_all | solution.py:13
  111.7 3.6 %all-to-all-start = ((bf16[256,8,512]{0,2,1:T(8,128)(2,1)}), bf16[256,8,512]{0,2,1:T(8,128)(2,1)S(1)}, u32[]{:S(2)}, u32[]{:S(2)}) async-start(bf16[256,8,512]{0,2,1:T(8,128)(2,1)} %bitcast.98), calls=%async_computation | async-start | bytes 4194304 | tf_op jit(solution)/shard_map/all_to_all | solution.py:30
  115.4 3.9 %copy.24 = bf16[256,8,512]{0,2,1:T(8,128)(2,1)} copy(bf16[256,8,512]{2,0,1:T(8,128)(2,1)} %bitcast.97) | data formatting | bytes 4194304 | tf_op jit(solution)/shard_map/reshape | solution.py:14
  119.6 22.3 %all-to-all-done = bf16[256,8,512]{0,2,1:T(8,128)(2,1)S(1)} async-done(((bf16[256,8,512]{0,2,1:T(8,128)(2,1)}), bf16[256,8,512]{0,2,1:T(8,128)(2,1)S(1)}, u32[]{:S(2)}, u32[]{:S(2)}) %all-to-all-start) | async-done | bytes 2097184 | tf_op jit(solution)/shard_map/all_to_all | solution.py:30
  141.9 2.9 %broadcast_select_fusion = (bf16[8,256,512]{1,2,0:T(8,128)(2,1)}, bf16[8,256,512]{1,2,0:T(8,128)(2,1)}, bf16[8,256,512]{1,2,0:T(8,128)(2,1)}) fusion(pred[8,256]{1,0:T(8,128)(4,1)S(1)} %bitcast.101, bf16[256,8,512]{0,2,1:T(8,128)(2,1)S(1)} %all-to-all-done, pred[8,256]{1,0:T(8,128)(4,1)S(1)} %bitcast.103, pred[8,256]{1,0:T(8,128)(4,1)S(1)} %bitcast.102), kind=kLoop, calls=%fused_computation.27 | loop fusion | flops 3145728 | bytes 8394752 | tf_op jit(solution)/shard_map/jit(_where)/select_n | solution.py:48
  144.8 3.9 %copy.19 = bf16[8,256,512]{2,1,0:T(8,128)(2,1)} copy(bf16[8,256,512]{1,2,0:T(8,128)(2,1)} %get-tuple-element.16) | data formatting | bytes 4194304 | tf_op jit(solution)/shard_map/jit(_where)/select_n | solution.py:48
  148.7 3.9 %copy.21 = bf16[8,256,512]{2,1,0:T(8,128)(2,1)} copy(bf16[8,256,512]{1,2,0:T(8,128)(2,1)} %get-tuple-element.17) | data formatting | bytes 4194304 | tf_op jit(solution)/shard_map/jit(_where)/select_n | solution.py:48
  152.7 3.9 %copy.23 = bf16[8,256,512]{2,1,0:T(8,128)(2,1)} copy(bf16[8,256,512]{1,2,0:T(8,128)(2,1)} %get-tuple-element.15) | data formatting | bytes 4194304 | tf_op jit(solution)/shard_map/jit(_where)/select_n | solution.py:48
  156.6 10.1 %fusion.26 = f32[2048,1536]{1,0:T(8,128)} fusion(bf16[2048,512]{1,0:T(8,128)(2,1)} %bitcast.99, bf16[3,512,1536]{2,1,0:T(8,128)(2,1)} %param.7), kind=kOutput, calls=%fused_computation.36 | convolution fusion | flops 3221225472 | bytes 16252928 | tf_op jit(solution)/shard_map/dot_general | solution.py:47
  166.8 7.9 %fusion.23 = f32[2048,1536]{1,0:T(8,128)} fusion(bf16[2048,512]{1,0:T(8,128)(2,1)S(1)} %bitcast.100, bf16[3,512,1536]{2,1,0:T(8,128)(2,1)} %param.7), kind=kOutput, calls=%fused_computation.33 | convolution fusion | flops 3221225472 | bytes 16252928 | tf_op jit(solution)/shard_map/dot_general | solution.py:47
  174.6 13.3 %add_convert_fusion = bf16[2048,1536]{1,0:T(8,128)(2,1)} fusion(f32[2048,1536]{1,0:T(8,128)} %fusion.26, f32[2048,1536]{1,0:T(8,128)} %fusion.23, bf16[2048,512]{1,0:T(8,128)(2,1)S(1)} %bitcast.95, bf16[3,512,1536]{2,1,0:T(8,128)(2,1)} %param.7), kind=kOutput, calls=%fused_computation | convolution fusion | flops 3230662656 | bytes 35127296 | tf_op jit(solution)/shard_map/dot_general | solution.py:47
  190.3 4.1 %bitcast_select_fusion.2 = (bf16[2048,512]{1,0:T(8,128)(2,1)S(1)}, bf16[2048,512]{1,0:T(8,128)(2,1)S(1)}, bf16[2048,512]{1,0:T(8,128)(2,1)S(1)}) fusion(bf16[8,256,512]{2,1,0:T(8,128)(2,1)} %copy.25, pred[2048]{0:T(1024)(128)(4,1)S(1)} %reshape.58, pred[2048]{0:T(1024)(128)(4,1)S(1)} %reshape.60, pred[2048]{0:T(1024)(128)(4,1)S(1)} %reshape.62), kind=kLoop, calls=%fused_computation.26 | loop fusion | flops 3145728 | bytes 8394752 | tf_op jit(solution)/shard_map/jit(_where)/select_n | solution.py:48
  194.4 7.4 %fusion.15 = bf16[1,512,1536]{2,1,0:T(8,128)(2,1)S(1)} fusion(bf16[2048,512]{1,0:T(8,128)(2,1)S(1)} %get-tuple-element.14, bf16[2048,1536]{1,0:T(8,128)(2,1)} %all-gather.7.cloned.1.call-done), kind=kOutput, calls=%fused_computation.21 | convolution fusion | flops 3222798336 | bytes 9961472 | tf_op jit(solution)/shard_map/dot_general | solution.py:59
  201.8 3.6 %fusion.16 = bf16[1,512,1536]{2,1,0:T(8,128)(2,1)S(1)} fusion(bf16[2048,512]{1,0:T(8,128)(2,1)S(1)} %get-tuple-element.13, bf16[2048,1536]{1,0:T(8,128)(2,1)S(1)} %bitcast.106), kind=kOutput, calls=%fused_computation.22 | convolution fusion | flops 3222798336 | bytes 9961472 | tf_op jit(solution)/shard_map/dot_general | solution.py:59
  205.4 3.6 %fusion.17 = bf16[1,512,1536]{2,1,0:T(8,128)(2,1)S(1)} fusion(bf16[2048,512]{1,0:T(8,128)(2,1)S(1)} %get-tuple-element.12, bf16[2048,1536]{1,0:T(8,128)(2,1)S(1)} %bitcast.106), kind=kOutput, calls=%fused_computation.23 | convolution fusion | flops 3222798336 | bytes 9961472 | tf_op jit(solution)/shard_map/dot_general | solution.py:59
  213.7 35.2 %reduce-scatter.3.cloned.1.call-done = bf16[256,1536]{1,0:T(8,128)(2,1)} async-done(((bf16[2048,1536]{1,0:T(8,128)(2,1)}), bf16[256,1536]{1,0:T(8,128)(2,1)}) %reduce-scatter.3.cloned.1.call-update) | async-done | bytes 786448 | tf_op jit(solution)/shard_map/reduce_scatter | solution.py:55
  (43 shorter events, 18.0 us)
Async XLA Ops:
  7.2 2.9 %copy-start.3 = (s32[8]{0:T(128)S(1)}, s32[8]{0:T(128)}, u32[]{:S(2)}) copy-start(s32[8]{0:T(128)} %param.9) | copy-start | bytes 100
  7.2 3.6 %copy-start.4 = (s32[256]{0:T(256)S(1)}, s32[256]{0:T(256)}, u32[]{:S(2)}) copy-start(s32[256]{0:T(256)} %param.8) | copy-start | bytes 3076
  7.2 50.8 %all-gather.7.cloned.1.call-start = ((), (), s32[]{:S(2)}) async-start(), calls=%async_computation.6 | async-start | bytes 7077888 | tf_op jit(solution)/shard_map/all_gather | solution.py:28
  7.9 97.9 %all-gather.5.cloned.1.call-start = ((), (), s32[]{:S(2)}) async-start(), calls=%async_computation.4 | async-start | bytes 2621440 | tf_op jit(solution)/shard_map/all_gather | solution.py:29
  58.0 6.3 %copy-start.5 = (bf16[2048,1536]{1,0:T(8,128)(2,1)S(1)}, bf16[2048,1536]{1,0:T(8,128)(2,1)}, u32[]{:S(2)}) copy-start(bf16[2048,1536]{1,0:T(8,128)(2,1)} %all-gather.7.cloned.1.call-done) | copy-start | bytes 18874372
  80.2 30.2 %all-to-all-start.1 = ((bf16[8,256,512]{2,1,0:T(8,128)(2,1)}), bf16[8,256,512]{2,1,0:T(8,128)(2,1)S(1)}, u32[]{:S(2)}, u32[]{:S(2)}) async-start(bf16[8,256,512]{2,1,0:T(8,128)(2,1)} %fusion.34), calls=%async_computation.2 | async-start | bytes 4194304 | tf_op jit(solution)/shard_map/all_to_all | solution.py:13
  110.4 1.3 copy-start.1
  111.7 30.2 %all-to-all-start = ((bf16[256,8,512]{0,2,1:T(8,128)(2,1)}), bf16[256,8,512]{0,2,1:T(8,128)(2,1)S(1)}, u32[]{:S(2)}, u32[]{:S(2)}) async-start(bf16[256,8,512]{0,2,1:T(8,128)(2,1)} %bitcast.98), calls=%async_computation | async-start | bytes 4194304 | tf_op jit(solution)/shard_map/all_to_all | solution.py:30
  115.3 96.2 %reduce-scatter.5.cloned.1.call-start = ((), (), s32[]{:S(2)}) async-start(), calls=%async_computation.7 | async-start | bytes 2621440 | tf_op jit(solution)/shard_map/reduce_scatter | solution.py:44
  119.3 129.6 %reduce-scatter.3.cloned.1.call-start = ((), (), s32[]{:S(2)}) async-start(), calls=%async_computation.5 | async-start | bytes 7077888 | tf_op jit(solution)/shard_map/reduce_scatter | solution.py:55
  156.6 10.1 %copy-start.2 = (bf16[8,256,512]{2,1,0:T(8,128)(2,1)S(1)}, bf16[8,256,512]{2,1,0:T(8,128)(2,1)}, u32[]{:S(2)}) copy-start(bf16[8,256,512]{2,1,0:T(8,128)(2,1)} %copy.21) | copy-start | bytes 6291460
  166.8 7.9 %copy-start = (bf16[8,256,512]{2,1,0:T(8,128)(2,1)S(1)}, bf16[8,256,512]{2,1,0:T(8,128)(2,1)}, u32[]{:S(2)}) copy-start(bf16[8,256,512]{2,1,0:T(8,128)(2,1)} %copy.23) | copy-start | bytes 6291460
  190.3 11.5 %slice-start = ((s8[6291456]{0:T(1024)(128)(4,1)}), s8[4194304]{0:T(1024)(128)(4,1)S(1)}, s32[]{:S(2)}) async-start(s8[6291456]{0:T(1024)(128)(4,1)} %bitcast.105), calls=%async_computation.8 | async-start | bytes 8388608
  194.4 7.4 %slice-start.1 = ((s8[6291456]{0:T(1024)(128)(4,1)}), s8[2097152]{0:T(1024)(128)(4,1)S(1)}, s32[]{:S(2)}) async-start(s8[6291456]{0:T(1024)(128)(4,1)} %bitcast.105), calls=%async_computation.9 | async-start | bytes 4194304
Sparse Core Ops, SparseCore 0:
  9.9 48.1 all-gather.6
  60.2 45.6 all-gather.4
  119.5 44.9 reduce-scatter.4
  188.1 60.8 reduce-scatter.2
